TPU v7x, 32 devices: a whole 2x2x4 slice. The times are simulated.
32 devices in a mesh: sub: 8 (over z, x), blk: 4 (over y, core).
Axes of the slice: x: 2, y: 2, z: 4, core: 2. Of those that a mesh axis runs over, the one named last changes fastest.
Arguments:
- a_tiles: bfloat16 [768, 12, 128, 128], P(('sub', 'blk'))
- modes: bfloat16 [768, 16, 128], P(('sub', 'blk')), may hold values from -6 to 6
- col_tiles: int32 [768, 12], P(('sub', 'blk')), may hold values from 0 to 221, as said below
- fetch_list: int32 [32, 126], P(('sub', 'blk')), may hold values from 0 to 767, as said below
Outputs:
- prolong: bfloat16 [768, 12, 16, 128], P(('sub', 'blk'))
- coarse_diag: float32 [768, 256], P('sub')
Inputs may be any that keep to these rules, and one draw needn't show every extreme that they name: `col_tiles`: slot 0 of row tile t names t itself (its index within its group); the other slots name other tiles of the same group (values below 96) or 96 + h for entry h of the device's fetch list; every entry of a device's fetch list is named by some slot of that device's rows. `fetch_list`: A device's list is 7 blocks of 18 entries; each block names distinct tiles of one group other than the device's own, different blocks name different groups; tile i of group g has number g * 96 + i.
All inputs are finite; a program needn't handle non-finite values.
Results may differ from a plain program's by a relative error of at most 0.008.
Values may be sent and summed in bfloat16 or wider, within the bound.
No kernel may reach another device: no remote copies, remote signals or barrier semaphores. Data moves between devices by JAX's collectives and lax.ppermute only.
A program may use at most 64 MiB of HBM per device.

v0:
```python
import jax
import jax.numpy as jnp
from jax import lax
from jax.sharding import PartitionSpec as P

NEIGHBOURS = 26
damping = 2.0 / 3.0


def shards(a_tiles, modes, col_tiles, fetch_list):
    blk_count = lax.axis_size("blk")
    sub_count = lax.axis_size("sub")
    tile_dev = a_tiles.shape[0]
    slot_count = a_tiles.shape[1]
    tile_rows = a_tiles.shape[2]
    mode_count = modes.shape[1]
    group_size = tile_dev * blk_count
    ghost_count = fetch_list.shape[1]
    peer_count = min(NEIGHBOURS, sub_count - 1)
    per_peer = ghost_count // peer_count
    group_modes = lax.all_gather(modes, "blk", axis=0, tiled=True)
    wanted = fetch_list[0].reshape(peer_count, per_peer)
    owners = wanted[:, 0] // group_size
    within = wanted % group_size
    selector = (owners[:, None] == jnp.arange(sub_count, dtype=jnp.int32)[None, :]).astype(
        jnp.int32
    )
    requests = jnp.sum(selector[:, :, None] * (within + 1)[:, None, :], axis=0)
    received = lax.all_to_all(requests, "sub", split_axis=0, concat_axis=0, tiled=True)
    present = received > 0
    picked = group_modes[jnp.maximum(received - 1, 0)]
    picked = jnp.where(present[:, :, None, None], picked, jnp.zeros_like(picked))
    returned = lax.all_to_all(picked, "sub", split_axis=0, concat_axis=0, tiled=True)
    returned, received = (returned, received)
    ghosts = returned[owners].reshape(ghost_count, mode_count, tile_rows)
    lookup = jnp.concatenate([group_modes, ghosts], axis=0)
    gathered = lookup[col_tiles]
    product = jnp.einsum("tkrc,tkmc->tkmr", a_tiles, gathered, preferred_element_type=jnp.float32)
    inverse = 1.0 / jnp.diagonal(a_tiles[:, 0], axis1=1, axis2=2).astype(jnp.float32)
    leading = (jnp.arange(slot_count) == 0).astype(jnp.float32)
    prolong = (
        leading[None, :, None, None] * modes.astype(jnp.float32)[:, None]
        - damping * inverse[:, None, None, :] * product
    ).astype(jnp.bfloat16)
    partial_value = (
        jnp.einsum(
            "tkmr,tknr->tkmn", prolong.astype(jnp.float32), product, precision=lax.Precision.HIGHEST
        )
        / tile_rows
    )
    partial_value = partial_value.reshape(tile_dev * slot_count, mode_count * mode_count)
    segment = (
        col_tiles.reshape(-1)[:, None]
        == jnp.arange(group_size + ghost_count, dtype=jnp.int32)[None, :]
    ).astype(jnp.float32)
    slot_sums = jnp.dot(
        segment.T,
        partial_value,
        precision=lax.Precision.HIGHEST,
        preferred_element_type=jnp.float32,
    )
    ghost_sums = slot_sums[group_size:].reshape(peer_count, per_peer, mode_count * mode_count)
    outgoing = jnp.einsum(
        "jp,jmv->pmv", selector.astype(jnp.float32), ghost_sums, precision=lax.Precision.HIGHEST
    )
    incoming = lax.all_to_all(
        outgoing.astype(jnp.bfloat16), "sub", split_axis=0, concat_axis=0, tiled=True
    ).astype(outgoing.dtype)
    target = (
        received[:, :, None] == jnp.arange(1, group_size + 1, dtype=jnp.int32)[None, None, :]
    ).astype(jnp.float32)
    local_sum = slot_sums[:group_size] + jnp.einsum(
        "pmg,pmv->gv", target, incoming, precision=lax.Precision.HIGHEST
    )
    coarse_diag = lax.psum(local_sum.astype(jnp.bfloat16), "blk").astype(jnp.float32)
    return (prolong, coarse_diag)


def solution(mesh):
    in_specs = (
        P(("sub", "blk"), None, None, None),
        P(("sub", "blk"), None, None),
        P(("sub", "blk"), None),
        P(("sub", "blk"), None),
    )
    out_specs = (P(("sub", "blk"), None, None, None), P("sub", None))
    return jax.shard_map(shards, mesh=mesh, in_specs=in_specs, out_specs=out_specs, check_vma=False)
```

profile of v0, /device:TPU:0, one launch (start us, length us, event | category | flops | bytes accessed | tf_op | source)
XLA Modules:
  0.0 80.3 jit_solution(5689057946343639641)
XLA Ops:
  0.6 0.5 broadcast.175
  1.2 1.3 %reduce.11 = s32[126]{0:T(128)S(1)} reduce(s32[1,126]{1,0:T(1,128)} %param.7, s32[]{:T(128)} %broadcast.175), dimensions={0}, to_apply=%param.7.reduce_sub_computation.3 | reduce | bytes 1012 | tf_op args[3]
  2.5 0.1 reshape_squeeze.3
  2.6 0.2 fusion.9
  2.7 0.1 copy.36
  2.8 0.7 multiply_reduce_fusion
  3.5 7.3 %all-to-all-start = ((s32[8,1,18]{2,1,0:T(1,128)}), s32[8,1,18]{2,1,0:T(1,128)S(1)}, u32[]{:S(2)}, u32[]{:S(2)}) async-start(s32[8,1,18]{2,1,0:T(1,128)} %bitcast.4), calls=%async_computation | async-start | bytes 8192 | tf_op jit(solution)/shard_map/all_to_all | solution.py:29
  10.8 6.7 %all_gather.3 = bf16[96,16,128]{2,1,0:T(8,128)(2,1)S(1)} all-gather(bf16[24,16,128]{2,1,0:T(8,128)(2,1)} %param.5), channel_id=1, replica_groups=mesh['sub'=8,'blk'=4] {'blk'}, dimensions={0}, use_global_device_ids=true | all-gather | bytes 491520 | tf_op jit(solution)/shard_map/all_gather | solution.py:21
  17.6 0.7 gather_fusion.1
  18.3 1.0 %broadcast_select_fusion = bf16[8,18,16,128]{3,2,1,0:T(8,128)(2,1)} fusion(bf16[8,18,16,128]{3,2,1,0:T(8,128)(2,1)S(1)} %bitcast.31, pred[8,18]{1,0:T(8,128)(4,1)S(1)} %broadcast_compare_fusion), kind=kLoop, calls=%fused_computation.11 | loop fusion | flops 294912 | bytes 1179792 | tf_op jit(solution)/shard_map/jit(_where)/select_n | solution.py:32
  19.4 6.0 %all-to-all-start.1 = ((bf16[8,18,16,128]{3,2,1,0:T(8,128)(2,1)}), bf16[8,18,16,128]{3,2,1,0:T(8,128)(2,1)S(1)}, u32[]{:S(2)}, u32[]{:S(2)}) async-start(bf16[8,18,16,128]{3,2,1,0:T(8,128)(2,1)} %broadcast_select_fusion), calls=%async_computation.1 | async-start | bytes 1179648 | tf_op jit(solution)/shard_map/all_to_all | solution.py:33
  25.4 3.2 %copy.42 = bf16[24,1,128,128]{0,3,2,1:T(8,128)(2,1)} copy(bf16[24,1,128,128]{3,2,1,0:T(8,128)(2,1)S(1)} %slice-done) | data formatting | bytes 1572864
  28.6 1.9 %gather_fusion = bf16[128,24]{1,0:T(8,128)(2,1)S(1)} fusion(bf16[24,128,128]{0,2,1:T(8,128)(2,1)} %bitcast.30, s32[128]{0:T(128)S(1)} %or_bitcast_fusion), kind=kCustom, calls=%fused_computation | custom fusion | bytes 13312 | tf_op jit(solution)/shard_map/jit(diagonal)/gather | solution.py:39
  30.7 0.1 copy.39
  30.8 0.1 copy.38
  30.9 0.1 reshape.117
  31.0 0.1 eq.58
  31.1 10.7 %all-to-all-done.1 = bf16[8,18,16,128]{3,2,1,0:T(8,128)(2,1)S(1)} async-done(((bf16[8,18,16,128]{3,2,1,0:T(8,128)(2,1)}), bf16[8,18,16,128]{3,2,1,0:T(8,128)(2,1)S(1)}, u32[]{:S(2)}, u32[]{:S(2)}) %all-to-all-start.1) | async-done | bytes 589856 | tf_op jit(solution)/shard_map/all_to_all | solution.py:33
  41.8 0.6 gather_fusion.2
  42.4 0.1 pad_maximum_fusion
  42.5 1.8 %gather_fusion.3 = bf16[288,16,128]{2,1,0:T(8,128)(2,1)S(1)} fusion(bf16[222,16,128]{2,1,0:T(8,128)(2,1)S(1)} %pad_maximum_fusion, s32[1024]{0:T(1024)S(1)} %pad_clamp_fusion), kind=kCustom, calls=%fused_computation.3 | custom fusion | bytes 2360448 | tf_op jit(solution)/shard_map/gather | solution.py:37
  44.4 7.5 %subtract_convert_fusion = (bf16[24,12,16,128]{3,2,1,0:T(8,128)(2,1)S(1)}, f32[24,12,16,128]{3,2,1,0:T(8,128)S(1)}) fusion(f32[24,128]{1,0:T(8,128)S(1)} %multiply_bitcast_fusion, f32[24,16,128]{2,1,0:T(8,128)S(1)} %convert_element_type.44, f32[12]{0:T(128)S(1)} %compare_convert_fusion, bf16[24,12,16,128]{3,2,1,0:T(8,128)(2,1)S(1)} %bitcast.29, ...), kind=kOutput, calls=%fused_computation.4 | convolution fusion | flops 153354240 | bytes 14364720 | tf_op jit(solution)/shard_map/tkrc,tkmc->tkmr/dot_general | solution.py:38
  51.8 2.0 %convolution_multiply_fusion = f32[24,12,16,16]{3,2,1,0:T(8,128)S(1)} fusion(bf16[24,12,16,128]{3,2,1,0:T(8,128)(2,1)S(1)} %get-tuple-element.4, f32[24,12,16,128]{3,2,1,0:T(8,128)S(1)} %get-tuple-element.5), kind=kOutput, calls=%fused_computation.5 | convolution fusion | flops 113319936 | bytes 3833856 | tf_op jit(solution)/shard_map/tkmr,tknr->tkmn/dot_general | solution.py:46
  53.8 1.7 %reshape.91 = f32[288,256]{1,0:T(8,128)} reshape(f32[24,12,16,16]{3,2,1,0:T(8,128)S(1)} %convolution_multiply_fusion) | data formatting | bytes 589824 | tf_op jit(solution)/shard_map/reshape | solution.py:51
  55.5 1.5 %fusion.2 = f32[222,256]{1,0:T(8,128)S(1)} fusion(f32[288,256]{1,0:T(8,128)} %reshape.91, s32[288]{0:T(512)S(1)} %eq.58), kind=kOutput, calls=%fused_computation.13 | convolution fusion | flops 196475328 | bytes 523392 | tf_op jit(solution)/shard_map/dot_general | solution.py:56
  57.1 0.3 convolution_convert_fusion
  57.4 0.7 copy.41
  58.0 3.6 %all-to-all-start.2 = ((bf16[8,18,256]{2,1,0:T(8,128)(2,1)}), bf16[8,18,256]{2,1,0:T(8,128)(2,1)S(1)}, u32[]{:S(2)}, u32[]{:S(2)}) async-start(bf16[8,18,256]{2,1,0:T(8,128)(2,1)} %copy.41), calls=%async_computation.2 | async-start | bytes 196608 | tf_op jit(solution)/shard_map/all_to_all | solution.py:66
  61.7 7.1 %all-to-all-done.2 = bf16[8,18,256]{2,1,0:T(8,128)(2,1)S(1)} async-done(((bf16[8,18,256]{2,1,0:T(8,128)(2,1)}), bf16[8,18,256]{2,1,0:T(8,128)(2,1)S(1)}, u32[]{:S(2)}, u32[]{:S(2)}) %all-to-all-start.2) | async-done | bytes 73760 | tf_op jit(solution)/shard_map/all_to_all | solution.py:66
  68.8 0.3 fusion.1
  69.1 10.5 %psum.7 = bf16[96,256]{1,0:T(8,128)(2,1)S(1)} all-reduce(bf16[96,256]{1,0:T(8,128)(2,1)S(1)} %fusion.1), channel_id=1, replica_groups=mesh['sub'=8,'blk'=4] {'blk'}, use_global_device_ids=true, to_apply=%region_1.2 | all-reduce | flops 24576 | bytes 98304 | tf_op jit(solution)/shard_map/psum | solution.py:75
  79.6 0.6 convert_element_type.51
  (26 shorter events, 0.3 us)
Async XLA Ops:
  0.6 24.7 %copy-start.1 = (bf16[24,16,128]{2,1,0:T(8,128)(2,1)S(1)}, bf16[24,16,128]{2,1,0:T(8,128)(2,1)}, u32[]{:S(2)}) copy-start(bf16[24,16,128]{2,1,0:T(8,128)(2,1)} %param.5) | copy-start | bytes 294916
  3.5 14.0 %all-to-all-start = ((s32[8,1,18]{2,1,0:T(1,128)}), s32[8,1,18]{2,1,0:T(1,128)S(1)}, u32[]{:S(2)}, u32[]{:S(2)}) async-start(s32[8,1,18]{2,1,0:T(1,128)} %bitcast.4), calls=%async_computation | async-start | bytes 8192 | tf_op jit(solution)/shard_map/all_to_all | solution.py:29
  18.3 7.1 %slice-start = ((bf16[24,12,128,128]{3,2,1,0:T(8,128)(2,1)}), bf16[24,1,128,128]{3,2,1,0:T(8,128)(2,1)S(1)}, s32[]{:S(2)}) async-start(bf16[24,12,128,128]{3,2,1,0:T(8,128)(2,1)} %param.4), calls=%async_computation.3 | async-start | bytes 1572864 | tf_op jit(solution)/shard_map/slice | solution.py:39
  19.4 22.4 %all-to-all-start.1 = ((bf16[8,18,16,128]{3,2,1,0:T(8,128)(2,1)}), bf16[8,18,16,128]{3,2,1,0:T(8,128)(2,1)S(1)}, u32[]{:S(2)}, u32[]{:S(2)}) async-start(bf16[8,18,16,128]{3,2,1,0:T(8,128)(2,1)} %broadcast_select_fusion), calls=%async_computation.1 | async-start | bytes 1179648 | tf_op jit(solution)/shard_map/all_to_all | solution.py:33
  25.4 5.3 %copy-start.2 = (s32[24,12]{0,1:T(8,128)S(1)}, s32[24,12]{0,1:T(8,128)}, u32[]{:S(2)}) copy-start(s32[24,12]{0,1:T(8,128)} %param.6) | copy-start | bytes 3460
  51.8 2.0 %copy-start = (bf16[24,12,16,128]{3,2,1,0:T(8,128)(2,1)}, bf16[24,12,16,128]{3,2,1,0:T(8,128)(2,1)S(1)}, u32[]{:S(2)}) copy-start(bf16[24,12,16,128]{3,2,1,0:T(8,128)(2,1)S(1)} %get-tuple-element.4) | copy-start | bytes 3538948
  58.0 10.8 %all-to-all-start.2 = ((bf16[8,18,256]{2,1,0:T(8,128)(2,1)}), bf16[8,18,256]{2,1,0:T(8,128)(2,1)S(1)}, u32[]{:S(2)}, u32[]{:S(2)}) async-start(bf16[8,18,256]{2,1,0:T(8,128)(2,1)} %copy.41), calls=%async_computation.2 | async-start | bytes 196608 | tf_op jit(solution)/shard_map/all_to_all | solution.py:66
where the time goes:
time: 80.7 us; the launch traced here: 80.3 us
  waiting for transfers between devices  17.8 us (22%)
  blocking collectives  17.2 us (21%)
  starting transfers between devices  16.9 us (21%)
  local copies, waits for them, and re-layouts  12 us (15%)
  matrix products  11.6 us (14%)
  other arithmetic  4.03 us (5%)
  between operations  0.83 us (1%)
    all_to_all x1, waiting for transfers between devices, shards(): lax.all_to_all(picked, 'sub', split_axis=0, concat_axis=0, tiled=True)  10.7 us
    psum x1, blocking collectives, shards(): lax.psum(local_sum.astype(jnp.bfloat16), 'blk').astype(jnp.float32)  10.5 us
    dot_general x1, matrix products, shards(): jnp.einsum('tkrc,tkmc->tkmr', a_tiles, gathered, preferred_element_type=j...  7.47 us
    all_to_all x1, starting transfers between devices, shards(): lax.all_to_all(requests, 'sub', split_axis=0, concat_axis=0, tiled=True)  7.28 us
    all_to_all x1, waiting for transfers between devices, shards(): lax.all_to_all(outgoing.astype(jnp.bfloat16), 'sub', split_axis=0, concat...  7.12 us
    all_gather x1, blocking collectives, shards(): group_modes = lax.all_gather(modes, 'blk', axis=0, tiled=True)  6.68 us
    all_to_all x1, starting transfers between devices, shards(): lax.all_to_all(picked, 'sub', split_axis=0, concat_axis=0, tiled=True)  5.99 us
    unnamed x9, local copies, waits for them, and re-layouts  3.84 us
  transfers between devices with their start and end apart: 3, of which 2 were waited for; matrix products, arithmetic and copies ran while one was open for 7% of the time, Pallas kernels for 0%

commit v1 on v0

--- a/solution.py
+++ b/solution.py
@@ -18,7 +18,22 @@
     ghost_count = fetch_list.shape[1]
     peer_count = min(NEIGHBOURS, sub_count - 1)
     per_peer = ghost_count // peer_count
-    group_modes = lax.all_gather(modes, "blk", axis=0, tiled=True)
+    ways, here, step = (lax.axis_size("blk"), lax.axis_index("blk"), modes.shape[0])
+    dims = [n * ways if d == 0 else n for d, n in enumerate(modes.shape)]
+    group_modes = lax.dynamic_update_slice_in_dim(
+        jnp.zeros(dims, modes.dtype), modes, here * step, axis=0
+    )
+    going_up = going_down = modes
+    for far in range(1, ways // 2 + 1):
+        going_up = lax.ppermute(going_up, "blk", [(d, (d + 1) % ways) for d in range(ways)])
+        group_modes = lax.dynamic_update_slice_in_dim(
+            group_modes, going_up, (here - far) % ways * step, axis=0
+        )
+        if 2 * far < ways:
+            going_down = lax.ppermute(going_down, "blk", [(d, (d - 1) % ways) for d in range(ways)])
+            group_modes = lax.dynamic_update_slice_in_dim(
+                group_modes, going_down, (here + far) % ways * step, axis=0
+            )
     wanted = fetch_list[0].reshape(peer_count, per_peer)
     owners = wanted[:, 0] // group_size
     within = wanted % group_size

time: 80.7 us -> 83.2 us (1.031)
  waiting for transfers between devices: 17.8 us -> 26.2 us
  blocking collectives: 17.2 us -> 10.8 us
  other arithmetic: 4.03 us -> 5.02 us
    all_gather x1 -> x0, blocking collectives: 6.68 us -> none  [shards(): group_modes = lax.all_gather(modes, 'blk', axis=0, tiled=True)]
    all_to_all x1, waiting for transfers between devices: 0.01 us -> 5.32 us  [shards(): lax.all_to_all(requests, 'sub', split_axis=0, concat_axis=0, tiled=True)]
    ppermute x0 -> x3, waiting for transfers between devices: none -> 3.97 us  [the longest x2 3.97 us: shards(): lax.ppermute(going_up, 'blk', [(d, (d + 1) % ways) for d in range(ways)])]
    ppermute x0 -> x3, starting transfers between devices: none -> 2.61 us  [the longest x1 2.01 us: shards(): lax.ppermute(going_down, 'blk', [(d, (d - 1) % ways) for d in range(ways)])]
    all_to_all x1, starting transfers between devices: 5.99 us -> 3.54 us  [shards(): lax.all_to_all(picked, 'sub', split_axis=0, concat_axis=0, tiled=True)]
    convert_element_type x1, other arithmetic: 0.02 us -> 1 us  [shards(): modes.astype(jnp.float32)[:, None]]
    all_to_all x1, waiting for transfers between devices: 10.7 us -> 9.77 us  [shards(): lax.all_to_all(picked, 'sub', split_axis=0, concat_axis=0, tiled=True)]
    unnamed x9 -> x7, local copies, waits for them, and re-layouts: 3.84 us -> 3.84 us
  transfers between devices with their start and end apart: 3 -> 6, of which waited for: 2 -> 4; matrix products, arithmetic and copies ran while one was open for 7% -> 12% of each run, Pallas kernels for 0% -> 0%
where the time goes in v1:
time: 83.2 us; the launch traced here: 82.8 us
  waiting for transfers between devices  26.2 us (31%)
  starting transfers between devices  16.3 us (20%)
  local copies, waits for them, and re-layouts  12.1 us (15%)
  matrix products  11.6 us (14%)
  blocking collectives  10.8 us (13%)
  other arithmetic  5.02 us (6%)
  between operations  0.91 us (1%)
    psum x1, blocking collectives, shards(): lax.psum(local_sum.astype(jnp.bfloat16), 'blk').astype(jnp.float32)  10.8 us
    all_to_all x1, waiting for transfers between devices, shards(): lax.all_to_all(picked, 'sub', split_axis=0, concat_axis=0, tiled=True)  9.77 us
    dot_general x1, matrix products, shards(): jnp.einsum('tkrc,tkmc->tkmr', a_tiles, gathered, preferred_element_type=j...  7.47 us
    all_to_all x1, waiting for transfers between devices, shards(): lax.all_to_all(outgoing.astype(jnp.bfloat16), 'sub', split_axis=0, concat...  7.12 us
    all_to_all x1, starting transfers between devices, shards(): lax.all_to_all(requests, 'sub', split_axis=0, concat_axis=0, tiled=True)  6.53 us
    all_to_all x1, waiting for transfers between devices, shards(): lax.all_to_all(requests, 'sub', split_axis=0, concat_axis=0, tiled=True)  5.32 us
    ppermute x2, waiting for transfers between devices, shards(): lax.ppermute(going_up, 'blk', [(d, (d + 1) % ways) for d in range(ways)])  3.97 us
    unnamed x7, local copies, waits for them, and re-layouts  3.84 us
  transfers between devices with their start and end apart: 6, of which 4 were waited for; matrix products, arithmetic and copies ran while one was open for 12% of the time, Pallas kernels for 0%

profile of v1, /device:TPU:0, one launch (start us, length us, event | category | flops | bytes accessed | tf_op | source)
XLA Modules:
  0.0 82.8 jit_solution(17203313170105914707)
XLA Ops:
  0.6 0.5 collective-permute-start
  1.2 2.0 %collective-permute-start.1 = (bf16[24,16,128]{2,1,0:T(8,128)(2,1)}, bf16[24,16,128]{2,1,0:T(8,128)(2,1)S(1)}, u32[]{:S(2)}, u32[]{:S(2)}) collective-permute-start(bf16[24,16,128]{2,1,0:T(8,128)(2,1)} %param.5), channel_id=1, source_target_pairs={{0,3},{1,0},{2,1},{3,2},{4,7},{5,4},{6,5},{7,6},{8,11},{9,8},{10,9... | collective-permute-start | bytes 294920 | tf_op jit(solution)/shard_map/ppermute | solution.py:33
  3.2 0.5 broadcast.178
  3.7 1.3 %reduce.11 = s32[126]{0:T(128)S(1)} reduce(s32[1,126]{1,0:T(1,128)} %param.7, s32[]{:T(128)} %broadcast.178), dimensions={0}, to_apply=%param.7.reduce_sub_computation.3 | reduce | bytes 1012 | tf_op args[3]
  5.1 0.2 fusion.9
  5.4 0.7 multiply_reduce_fusion
  6.0 6.5 %all-to-all-start = ((s32[8,1,18]{2,1,0:T(1,128)}), s32[8,1,18]{2,1,0:T(1,128)S(1)}, u32[]{:S(2)}, u32[]{:S(2)}) async-start(s32[8,1,18]{2,1,0:T(1,128)} %bitcast.4), calls=%async_computation | async-start | bytes 8192 | tf_op jit(solution)/shard_map/all_to_all | solution.py:44
  12.6 1.0 %fusion.16 = (f32[24,16,128]{2,1,0:T(8,128)S(1)}, bf16[96,16,128]{2,1,0:T(8,128)(2,1)S(1)}) fusion(bf16[24,16,128]{2,1,0:T(8,128)(2,1)} %param.5, bf16[96,16,128]{2,1,0:T(8,128)(2,1)S(1)} %broadcast_in_dim.16, s32[]{:T(128)S(6)} %select_n.62), kind=kLoop, calls=%fused_computation.47 | loop fusion | flops 49152 | bytes 393220 | tf_op jit(solution)/shard_map/convert_element_type | solution.py:57
  13.7 5.3 %all-to-all-done = s32[8,1,18]{2,1,0:T(1,128)S(1)} async-done(((s32[8,1,18]{2,1,0:T(1,128)}), s32[8,1,18]{2,1,0:T(1,128)S(1)}, u32[]{:S(2)}, u32[]{:S(2)}) %all-to-all-start) | async-done | bytes 608 | tf_op jit(solution)/shard_map/all_to_all | solution.py:44
  19.2 4.0 %collective-permute-done.2 = bf16[24,16,128]{2,1,0:T(8,128)(2,1)S(1)} collective-permute-done((bf16[24,16,128]{2,1,0:T(8,128)(2,1)S(1)}, bf16[24,16,128]{2,1,0:T(8,128)(2,1)S(1)}, u32[]{:S(2)}, u32[]{:S(2)}) %collective-permute-start.2) | collective-permute-done | bytes 98336 | tf_op jit(solution)/shard_map/ppermute | solution.py:28
  23.2 0.7 gather_fusion.1
  24.0 1.0 %broadcast_select_fusion = bf16[8,18,16,128]{3,2,1,0:T(8,128)(2,1)} fusion(bf16[8,18,16,128]{3,2,1,0:T(8,128)(2,1)S(1)} %bitcast.31, pred[8,18]{1,0:T(8,128)(4,1)S(1)} %broadcast_compare_fusion), kind=kLoop, calls=%fused_computation.11 | loop fusion | flops 294912 | bytes 1179792 | tf_op jit(solution)/shard_map/jit(_where)/select_n | solution.py:47
  25.0 3.5 %all-to-all-start.1 = ((bf16[8,18,16,128]{3,2,1,0:T(8,128)(2,1)}), bf16[8,18,16,128]{3,2,1,0:T(8,128)(2,1)S(1)}, u32[]{:S(2)}, u32[]{:S(2)}) async-start(bf16[8,18,16,128]{3,2,1,0:T(8,128)(2,1)} %broadcast_select_fusion), calls=%async_computation.1 | async-start | bytes 1179648 | tf_op jit(solution)/shard_map/all_to_all | solution.py:48
  28.6 3.2 %copy.42 = bf16[24,1,128,128]{0,3,2,1:T(8,128)(2,1)} copy(bf16[24,1,128,128]{3,2,1,0:T(8,128)(2,1)S(1)} %slice-done) | data formatting | bytes 1572864
  31.8 1.9 %gather_fusion = bf16[128,24]{1,0:T(8,128)(2,1)S(1)} fusion(bf16[24,128,128]{0,2,1:T(8,128)(2,1)} %bitcast.30, s32[128]{0:T(128)S(1)} %or_bitcast_fusion), kind=kCustom, calls=%fused_computation | custom fusion | bytes 13312 | tf_op jit(solution)/shard_map/jit(diagonal)/gather | solution.py:54
  33.8 0.1 copy.39
  34.0 0.1 reshape.117
  34.1 0.1 eq.62
  34.3 9.8 %all-to-all-done.1 = bf16[8,18,16,128]{3,2,1,0:T(8,128)(2,1)S(1)} async-done(((bf16[8,18,16,128]{3,2,1,0:T(8,128)(2,1)}), bf16[8,18,16,128]{3,2,1,0:T(8,128)(2,1)S(1)}, u32[]{:S(2)}, u32[]{:S(2)}) %all-to-all-start.1) | async-done | bytes 589856 | tf_op jit(solution)/shard_map/all_to_all | solution.py:48
  44.1 0.6 gather_fusion.2
  44.8 1.8 %gather_fusion.3 = bf16[288,16,128]{2,1,0:T(8,128)(2,1)S(1)} fusion(bf16[222,16,128]{2,1,0:T(8,128)(2,1)S(1)} %pad_maximum_fusion, s32[1024]{0:T(1024)S(1)} %pad_clamp_fusion), kind=kCustom, calls=%fused_computation.3 | custom fusion | bytes 2360448 | tf_op jit(solution)/shard_map/gather | solution.py:52
  46.6 7.5 %subtract_convert_fusion = (bf16[24,12,16,128]{3,2,1,0:T(8,128)(2,1)S(1)}, f32[24,12,16,128]{3,2,1,0:T(8,128)S(1)}) fusion(f32[24,128]{1,0:T(8,128)S(1)} %multiply_bitcast_fusion, f32[24,16,128]{2,1,0:T(8,128)S(1)} %get-tuple-element.4, f32[12]{0:T(128)S(1)} %compare_convert_fusion, bf16[24,12,16,128]{3,2,1,0:T(8,128)(2,1)S(1)} %bitcast.29, ...), kind=kOutput, calls=%fused_computation.4 | convolution fusion | flops 153354240 | bytes 14364720 | tf_op jit(solution)/shard_map/tkrc,tkmc->tkmr/dot_general | solution.py:53
  54.1 2.0 %convolution_multiply_fusion = f32[24,12,16,16]{3,2,1,0:T(8,128)S(1)} fusion(bf16[24,12,16,128]{3,2,1,0:T(8,128)(2,1)S(1)} %get-tuple-element.6, f32[24,12,16,128]{3,2,1,0:T(8,128)S(1)} %get-tuple-element.7), kind=kOutput, calls=%fused_computation.5 | convolution fusion | flops 113319936 | bytes 3833856 | tf_op jit(solution)/shard_map/tkmr,tknr->tkmn/dot_general | solution.py:61
  56.1 1.7 %reshape.91 = f32[288,256]{1,0:T(8,128)} reshape(f32[24,12,16,16]{3,2,1,0:T(8,128)S(1)} %convolution_multiply_fusion) | data formatting | bytes 589824 | tf_op jit(solution)/shard_map/reshape | solution.py:66
  57.8 1.5 %fusion.2 = f32[222,256]{1,0:T(8,128)S(1)} fusion(f32[288,256]{1,0:T(8,128)} %reshape.91, s32[288]{0:T(512)S(1)} %eq.62), kind=kOutput, calls=%fused_computation.13 | convolution fusion | flops 196475328 | bytes 523392 | tf_op jit(solution)/shard_map/dot_general | solution.py:71
  59.4 0.3 convolution_convert_fusion
  59.7 0.7 copy.41
  60.3 3.6 %all-to-all-start.2 = ((bf16[8,18,256]{2,1,0:T(8,128)(2,1)}), bf16[8,18,256]{2,1,0:T(8,128)(2,1)S(1)}, u32[]{:S(2)}, u32[]{:S(2)}) async-start(bf16[8,18,256]{2,1,0:T(8,128)(2,1)} %copy.41), calls=%async_computation.2 | async-start | bytes 196608 | tf_op jit(solution)/shard_map/all_to_all | solution.py:81
  63.9 7.1 %all-to-all-done.2 = bf16[8,18,256]{2,1,0:T(8,128)(2,1)S(1)} async-done(((bf16[8,18,256]{2,1,0:T(8,128)(2,1)}), bf16[8,18,256]{2,1,0:T(8,128)(2,1)S(1)}, u32[]{:S(2)}, u32[]{:S(2)}) %all-to-all-start.2) | async-done | bytes 73760 | tf_op jit(solution)/shard_map/all_to_all | solution.py:81
  71.0 0.3 fusion.1
  71.3 10.8 %psum.7 = bf16[96,256]{1,0:T(8,128)(2,1)S(1)} all-reduce(bf16[96,256]{1,0:T(8,128)(2,1)S(1)} %fusion.1), channel_id=1, replica_groups=mesh['sub'=8,'blk'=4] {'blk'}, use_global_device_ids=true, to_apply=%region_1.2 | all-reduce | flops 24576 | bytes 98304 | tf_op jit(solution)/shard_map/psum | solution.py:90
  82.1 0.6 convert_element_type.51
  (33 shorter events, 0.8 us)
Async XLA Ops:
  0.6 18.5 %collective-permute-start = (bf16[24,16,128]{2,1,0:T(8,128)(2,1)}, bf16[24,16,128]{2,1,0:T(8,128)(2,1)S(1)}, u32[]{:S(2)}, u32[]{:S(2)}) collective-permute-start(bf16[24,16,128]{2,1,0:T(8,128)(2,1)} %param.5), channel_id=1, source_target_pairs={{0,1},{1,2},{2,3},{3,0},{4,5},{5,6},{6,7},{7,4},{8,9},{9,10},{10,1... | collective-permute-start | bytes 294920 | tf_op jit(solution)/shard_map/ppermute | solution.py:28
  1.2 18.0 %collective-permute-start.1 = (bf16[24,16,128]{2,1,0:T(8,128)(2,1)}, bf16[24,16,128]{2,1,0:T(8,128)(2,1)S(1)}, u32[]{:S(2)}, u32[]{:S(2)}) collective-permute-start(bf16[24,16,128]{2,1,0:T(8,128)(2,1)} %param.5), channel_id=1, source_target_pairs={{0,3},{1,0},{2,1},{3,2},{4,7},{5,4},{6,5},{7,6},{8,11},{9,8},{10,9... | collective-permute-start | bytes 294920 | tf_op jit(solution)/shard_map/ppermute | solution.py:33
  6.0 12.9 %all-to-all-start = ((s32[8,1,18]{2,1,0:T(1,128)}), s32[8,1,18]{2,1,0:T(1,128)S(1)}, u32[]{:S(2)}, u32[]{:S(2)}) async-start(s32[8,1,18]{2,1,0:T(1,128)} %bitcast.4), calls=%async_computation | async-start | bytes 8192 | tf_op jit(solution)/shard_map/all_to_all | solution.py:44
  19.1 4.1 %collective-permute-start.2 = (bf16[24,16,128]{2,1,0:T(8,128)(2,1)S(1)}, bf16[24,16,128]{2,1,0:T(8,128)(2,1)S(1)}, u32[]{:S(2)}, u32[]{:S(2)}) collective-permute-start(bf16[24,16,128]{2,1,0:T(8,128)(2,1)S(1)} %collective-permute-done), channel_id=1, source_target_pairs={{0,1},{1,2},{2,3},{3,0},{4,5},{5,6},{6,7},{7,4},{8,9},{9,10},{10,1... | collective-permute-start | bytes 294920 | tf_op jit(solution)/shard_map/ppermute | solution.py:28
  23.2 5.3 %slice-start = ((bf16[24,12,128,128]{3,2,1,0:T(8,128)(2,1)}), bf16[24,1,128,128]{3,2,1,0:T(8,128)(2,1)S(1)}, s32[]{:S(2)}) async-start(bf16[24,12,128,128]{3,2,1,0:T(8,128)(2,1)} %param.4), calls=%async_computation.3 | async-start | bytes 1572864 | tf_op jit(solution)/shard_map/slice | solution.py:54
  25.0 19.0 %all-to-all-start.1 = ((bf16[8,18,16,128]{3,2,1,0:T(8,128)(2,1)}), bf16[8,18,16,128]{3,2,1,0:T(8,128)(2,1)S(1)}, u32[]{:S(2)}, u32[]{:S(2)}) async-start(bf16[8,18,16,128]{3,2,1,0:T(8,128)(2,1)} %broadcast_select_fusion), calls=%async_computation.1 | async-start | bytes 1179648 | tf_op jit(solution)/shard_map/all_to_all | solution.py:48
  28.6 5.3 %copy-start.1 = (s32[24,12]{0,1:T(8,128)S(1)}, s32[24,12]{0,1:T(8,128)}, u32[]{:S(2)}) copy-start(s32[24,12]{0,1:T(8,128)} %param.6) | copy-start | bytes 3460
  54.1 2.0 %copy-start = (bf16[24,12,16,128]{3,2,1,0:T(8,128)(2,1)}, bf16[24,12,16,128]{3,2,1,0:T(8,128)(2,1)S(1)}, u32[]{:S(2)}) copy-start(bf16[24,12,16,128]{3,2,1,0:T(8,128)(2,1)S(1)} %get-tuple-element.6) | copy-start | bytes 3538948
  60.3 10.7 %all-to-all-start.2 = ((bf16[8,18,256]{2,1,0:T(8,128)(2,1)}), bf16[8,18,256]{2,1,0:T(8,128)(2,1)S(1)}, u32[]{:S(2)}, u32[]{:S(2)}) async-start(bf16[8,18,256]{2,1,0:T(8,128)(2,1)} %copy.41), calls=%async_computation.2 | async-start | bytes 196608 | tf_op jit(solution)/shard_map/all_to_all | solution.py:81
